TPU v7x, 256 devices: a whole 4x4x8 slice. The times are simulated.
256 devices in a mesh: panel: 8 (over z), rows: 32 (over y, x, core).
Axes of the slice: x: 4, y: 4, z: 8, core: 2. Of those that a mesh axis runs over, the one named last changes fastest.
Arguments:
- rhs_diag: bfloat16 [8, 8192, 128], P(None, 'rows'), may hold values from -6 to 6
- rhs_tall: bfloat16 [8, 16384, 128], P('panel', 'rows'), may hold values from -6 to 6
- diag_inverse: bfloat16 [8, 1024, 1024], P('panel'), may hold values from -0.1875 to 0.1875
- coupling: bfloat16 [8, 8192, 1024], P('panel', 'rows'), may hold values from -0.09375 to 0.09375
- tall_blocks: bfloat16 [8, 128, 128, 1024], P('panel', 'rows'), may hold values from -0.125 to 0.125
- sparsity: int32 [128, 8], P('rows', 'panel'), may hold values 0 or 1
Outputs:
- solution: float32 [8, 8, 1024, 128], P('panel', None, 'rows')
- tall_residual: float32 [8, 16384, 128], P('panel', 'rows')
All inputs are finite; a program needn't handle non-finite values. No bound on the sum of `sparsity` on one device may be relied on, other than what follows from the above.
Results may differ from a plain program's by a relative error of at most 0.0085.
Values may be sent and summed in bfloat16 or wider, within the bound.
No kernel may reach another device: no remote copies, remote signals or barrier semaphores. Data moves between devices by JAX's collectives and lax.ppermute only.
A program may use at most 64 MiB of HBM per device.

v0:
```python
import jax
import jax.numpy as jnp
from jax import lax
from jax.sharding import PartitionSpec as P


def shifted(block, axis, distance):
    devices = range(lax.axis_size(axis))
    route = [(i - distance, i) for i in devices if i - distance in devices]
    return lax.ppermute(block, axis, route)


def per_device(rhs_diag, rhs_tall, diag_inverse, coupling, tall_blocks, sparsity):
    panel_index = lax.axis_index("panel")
    rows_index = lax.axis_index("rows")
    panel_count = lax.axis_size("panel")
    rows_count = lax.axis_size("rows")
    batches, rows_here, columns = rhs_diag.shape
    panel_width = diag_inverse.shape[1]
    slice_rows = panel_width // rows_count
    blocks_here = tall_blocks.shape[1]
    block_rows = tall_blocks.shape[2]
    tall_rows = blocks_here * block_rows
    rows_panel = rows_index * rows_here // panel_width
    offset = jnp.clip(
        rows_index * rows_here - panel_index * panel_width, 0, panel_width - rows_here
    )
    inverse_cols = lax.dynamic_slice_in_dim(diag_inverse[0], offset, rows_here, 1)
    owner = rows_panel == panel_index
    is_later = rows_panel > panel_index
    coupling_here = coupling[0]
    tall_matrix = tall_blocks[0].reshape(tall_rows, panel_width)
    block_mask = jnp.repeat(sparsity[:, 0].astype(jnp.float32), block_rows)[:, None]

    def advance(tick_number, state_now):
        incoming, solutions, stored = state_now
        batch_now = tick_number - panel_index
        active = (batch_now >= 0) & (batch_now < batches)
        batch_safe = jnp.clip(batch_now, 0, batches - 1)
        rhs_now = lax.dynamic_index_in_dim(rhs_diag, batch_safe, 0, keepdims=False).astype(
            jnp.float32
        )
        reduced = (rhs_now - incoming).astype(jnp.bfloat16)
        partial_value = jnp.dot(inverse_cols, reduced, preferred_element_type=jnp.float32)
        partial_value = jnp.where(owner, partial_value, jnp.float32(0.0))
        summed_all = lax.psum(partial_value, "rows")
        own_rows = lax.dynamic_slice_in_dim(summed_all, rows_index * slice_rows, slice_rows, 0)
        solved = summed_all.astype(jnp.bfloat16)
        previous = lax.dynamic_index_in_dim(solutions, batch_safe, 0, keepdims=False)
        solutions = lax.dynamic_update_index_in_dim(
            solutions, jnp.where(active, own_rows, previous), batch_safe, 0
        )
        update = jnp.dot(coupling_here, solved, preferred_element_type=jnp.float32)
        outgoing = incoming + jnp.where(is_later, update, jnp.float32(0.0))
        earlier = lax.dynamic_index_in_dim(stored, batch_safe, 0, keepdims=False)
        stored = lax.dynamic_update_index_in_dim(
            stored, jnp.where(active, solved, earlier), batch_safe, 0
        )
        incoming = shifted(outgoing, "panel", 1)
        return (incoming, solutions, stored)

    stored = jnp.zeros((batches, panel_width, columns), jnp.bfloat16)
    initial = (
        jnp.zeros((rows_here, columns), jnp.float32),
        jnp.zeros((batches, slice_rows, columns), jnp.float32),
        stored,
    )
    tick_count = batches + panel_count - 1
    incoming, solutions, stored = lax.fori_loop(0, tick_count, advance, initial)
    tall_terms = (
        jnp.einsum("rw,bws->brs", tall_matrix, stored, preferred_element_type=jnp.float32)
        * block_mask
    )
    summed = lax.psum_scatter(tall_terms, "panel", scatter_dimension=0, tiled=True)
    tall_residual = rhs_tall.astype(jnp.float32) - summed
    return (solutions[None], tall_residual)


def solution(mesh):
    placed = (
        P(None, "rows", None),
        P("panel", "rows", None),
        P("panel", None, None),
        P("panel", "rows", None),
        P("panel", "rows", None, None),
        P("rows", "panel"),
    )
    return jax.shard_map(
        per_device,
        mesh=mesh,
        in_specs=placed,
        out_specs=(P("panel", None, "rows", None), P("panel", "rows", None)),
        check_vma=False,
    )
```

profile of v0, /device:TPU:2, one launch (start us, length us, event | category | flops | bytes accessed | tf_op | source)
XLA Modules:
  0.0 1989.9 jit_solution(4910491097746578890)
XLA Ops:
  9.9 1.6 broadcast_in_dim.57
  12.2 1919.9 %while.19 = (s32[]{:T(128)}, f32[256,128]{0,1:T(8,128)S(1)}, f32[8,32,128]{2,1,0:T(8,128)}, bf16[8,1024,128]{1,2,0:T(8,128)(2,1)}, pred[]{:T(512)}, /*index=5*/p...) while((s32[]{:T(128)}, f32[256,128]{0,1:T(8,128)S(1)}, ...), condition=%wide.region_2.3_spmd, body=%wide.region_0.2_spmd.sunk | while | flops 135041024 | bytes 8307022 | solution.py:69
  16.7 115.6 %all-reduce.2.cloned.1.call-done = f32[1024,128]{0,1:T(8,128)} async-done(((f32[1024,128]{0,1:T(8,128)}), f32[1024,128]{0,1:T(8,128)}) %all-reduce.2.cloned.1.call-update) | async-done | bytes 524304 | tf_op jit(solution)/shard_map/while/body/eval_jaxpr/psum | solution.py:46
  132.3 2.0 fusion.24
  134.3 3.5 collective-permute-start
  137.8 1.8 bitcast_dynamic-update-slice_fusion.2
  145.8 114.6 %all-reduce.2.cloned.1.call-done = f32[1024,128]{0,1:T(8,128)} async-done(((f32[1024,128]{0,1:T(8,128)}), f32[1024,128]{0,1:T(8,128)}) %all-reduce.2.cloned.1.call-update) | async-done | bytes 524304 | tf_op jit(solution)/shard_map/while/body/eval_jaxpr/psum | solution.py:46
  260.4 2.0 fusion.24
  262.4 3.5 collective-permute-start
  265.9 1.8 bitcast_dynamic-update-slice_fusion.2
  273.9 114.6 %all-reduce.2.cloned.1.call-done = f32[1024,128]{0,1:T(8,128)} async-done(((f32[1024,128]{0,1:T(8,128)}), f32[1024,128]{0,1:T(8,128)}) %all-reduce.2.cloned.1.call-update) | async-done | bytes 524304 | tf_op jit(solution)/shard_map/while/body/eval_jaxpr/psum | solution.py:46
  388.5 2.0 fusion.24
  390.5 3.5 collective-permute-start
  394.0 1.8 bitcast_dynamic-update-slice_fusion.2
  401.9 114.3 %all-reduce.2.cloned.1.call-done = f32[1024,128]{0,1:T(8,128)} async-done(((f32[1024,128]{0,1:T(8,128)}), f32[1024,128]{0,1:T(8,128)}) %all-reduce.2.cloned.1.call-update) | async-done | bytes 524304 | tf_op jit(solution)/shard_map/while/body/eval_jaxpr/psum | solution.py:46
  516.2 2.0 fusion.24
  518.2 3.5 collective-permute-start
  521.7 1.8 bitcast_dynamic-update-slice_fusion.2
  529.7 114.3 %all-reduce.2.cloned.1.call-done = f32[1024,128]{0,1:T(8,128)} async-done(((f32[1024,128]{0,1:T(8,128)}), f32[1024,128]{0,1:T(8,128)}) %all-reduce.2.cloned.1.call-update) | async-done | bytes 524304 | tf_op jit(solution)/shard_map/while/body/eval_jaxpr/psum | solution.py:46
  644.0 2.0 fusion.24
  646.0 3.5 collective-permute-start
  649.5 1.8 bitcast_dynamic-update-slice_fusion.2
  657.5 114.2 %all-reduce.2.cloned.1.call-done = f32[1024,128]{0,1:T(8,128)} async-done(((f32[1024,128]{0,1:T(8,128)}), f32[1024,128]{0,1:T(8,128)}) %all-reduce.2.cloned.1.call-update) | async-done | bytes 524304 | tf_op jit(solution)/shard_map/while/body/eval_jaxpr/psum | solution.py:46
  771.7 2.0 fusion.24
  773.7 3.5 collective-permute-start
  777.2 1.8 bitcast_dynamic-update-slice_fusion.2
  785.2 114.6 %all-reduce.2.cloned.1.call-done = f32[1024,128]{0,1:T(8,128)} async-done(((f32[1024,128]{0,1:T(8,128)}), f32[1024,128]{0,1:T(8,128)}) %all-reduce.2.cloned.1.call-update) | async-done | bytes 524304 | tf_op jit(solution)/shard_map/while/body/eval_jaxpr/psum | solution.py:46
  899.8 2.0 fusion.24
  901.8 3.5 collective-permute-start
  905.3 1.8 bitcast_dynamic-update-slice_fusion.2
  913.2 114.6 %all-reduce.2.cloned.1.call-done = f32[1024,128]{0,1:T(8,128)} async-done(((f32[1024,128]{0,1:T(8,128)}), f32[1024,128]{0,1:T(8,128)}) %all-reduce.2.cloned.1.call-update) | async-done | bytes 524304 | tf_op jit(solution)/shard_map/while/body/eval_jaxpr/psum | solution.py:46
  1027.8 2.0 fusion.24
  1029.8 3.5 collective-permute-start
  1033.3 1.8 bitcast_dynamic-update-slice_fusion.2
  1041.3 114.6 %all-reduce.2.cloned.1.call-done = f32[1024,128]{0,1:T(8,128)} async-done(((f32[1024,128]{0,1:T(8,128)}), f32[1024,128]{0,1:T(8,128)}) %all-reduce.2.cloned.1.call-update) | async-done | bytes 524304 | tf_op jit(solution)/shard_map/while/body/eval_jaxpr/psum | solution.py:46
  1155.9 2.0 fusion.24
  1157.9 3.5 collective-permute-start
  1161.4 1.8 bitcast_dynamic-update-slice_fusion.2
  1169.4 114.3 %all-reduce.2.cloned.1.call-done = f32[1024,128]{0,1:T(8,128)} async-done(((f32[1024,128]{0,1:T(8,128)}), f32[1024,128]{0,1:T(8,128)}) %all-reduce.2.cloned.1.call-update) | async-done | bytes 524304 | tf_op jit(solution)/shard_map/while/body/eval_jaxpr/psum | solution.py:46
  1283.6 2.0 fusion.24
  1285.7 3.5 collective-permute-start
  1289.1 1.8 bitcast_dynamic-update-slice_fusion.2
  1297.1 114.6 %all-reduce.2.cloned.1.call-done = f32[1024,128]{0,1:T(8,128)} async-done(((f32[1024,128]{0,1:T(8,128)}), f32[1024,128]{0,1:T(8,128)}) %all-reduce.2.cloned.1.call-update) | async-done | bytes 524304 | tf_op jit(solution)/shard_map/while/body/eval_jaxpr/psum | solution.py:46
  1411.7 2.0 fusion.24
  1413.8 3.5 collective-permute-start
  1417.2 1.8 bitcast_dynamic-update-slice_fusion.2
  1425.2 114.3 %all-reduce.2.cloned.1.call-done = f32[1024,128]{0,1:T(8,128)} async-done(((f32[1024,128]{0,1:T(8,128)}), f32[1024,128]{0,1:T(8,128)}) %all-reduce.2.cloned.1.call-update) | async-done | bytes 524304 | tf_op jit(solution)/shard_map/while/body/eval_jaxpr/psum | solution.py:46
  1539.5 2.0 fusion.24
  1541.6 3.5 collective-permute-start
  1545.0 1.8 bitcast_dynamic-update-slice_fusion.2
  1553.0 114.6 %all-reduce.2.cloned.1.call-done = f32[1024,128]{0,1:T(8,128)} async-done(((f32[1024,128]{0,1:T(8,128)}), f32[1024,128]{0,1:T(8,128)}) %all-reduce.2.cloned.1.call-update) | async-done | bytes 524304 | tf_op jit(solution)/shard_map/while/body/eval_jaxpr/psum | solution.py:46
  1667.6 2.0 fusion.24
  1669.6 3.5 collective-permute-start
  1673.1 1.8 bitcast_dynamic-update-slice_fusion.2
  1681.0 114.2 %all-reduce.2.cloned.1.call-done = f32[1024,128]{0,1:T(8,128)} async-done(((f32[1024,128]{0,1:T(8,128)}), f32[1024,128]{0,1:T(8,128)}) %all-reduce.2.cloned.1.call-update) | async-done | bytes 524304 | tf_op jit(solution)/shard_map/while/body/eval_jaxpr/psum | solution.py:46
  1795.3 2.0 fusion.24
  1797.3 3.5 collective-permute-start
  1800.8 1.8 bitcast_dynamic-update-slice_fusion.2
  1808.8 114.3 %all-reduce.2.cloned.1.call-done = f32[1024,128]{0,1:T(8,128)} async-done(((f32[1024,128]{0,1:T(8,128)}), f32[1024,128]{0,1:T(8,128)}) %all-reduce.2.cloned.1.call-update) | async-done | bytes 524304 | tf_op jit(solution)/shard_map/while/body/eval_jaxpr/psum | solution.py:46
  1923.1 2.0 fusion.24
  1925.1 3.5 collective-permute-start
  1928.6 1.8 bitcast_dynamic-update-slice_fusion.2
  1932.0 4.5 multiply_bitcast_fusion
  1937.5 43.4 %reduce-scatter.2.cloned.1.call-done = f32[1,512,128]{1,2,0:T(8,128)} async-done(((f32[8,512,128]{1,2,0:T(8,128)}), f32[1,512,128]{1,2,0:T(8,128)}) %reduce-scatter.2.cloned.1.call-update) | async-done | bytes 262160 | tf_op jit(solution)/shard_map/reduce_scatter | solution.py:74
  (226 shorter events, 97.2 us)
Async XLA Ops:
  8.0 1.6 copy-start
  8.0 4.1 copy-start.1
  12.2 120.1 %all-reduce.2.cloned.1.call-start = ((), (), s32[]{:S(2)}) async-start(), calls=%async_computation.2 | async-start | bytes 1048576 | tf_op jit(solution)/shard_map/while/body/eval_jaxpr/psum | solution.py:46
  132.3 7.3 copy-start.2
  134.3 6.9 collective-permute-start
  141.2 119.2 %all-reduce.2.cloned.1.call-start = ((), (), s32[]{:S(2)}) async-start(), calls=%async_computation.2 | async-start | bytes 1048576 | tf_op jit(solution)/shard_map/while/body/eval_jaxpr/psum | solution.py:46
  260.4 7.3 copy-start.2
  262.4 6.9 collective-permute-start
  269.3 119.1 %all-reduce.2.cloned.1.call-start = ((), (), s32[]{:S(2)}) async-start(), calls=%async_computation.2 | async-start | bytes 1048576 | tf_op jit(solution)/shard_map/while/body/eval_jaxpr/psum | solution.py:46
  388.5 7.3 copy-start.2
  390.5 6.9 collective-permute-start
  397.4 118.8 %all-reduce.2.cloned.1.call-start = ((), (), s32[]{:S(2)}) async-start(), calls=%async_computation.2 | async-start | bytes 1048576 | tf_op jit(solution)/shard_map/while/body/eval_jaxpr/psum | solution.py:46
  516.2 7.3 copy-start.2
  518.2 6.9 collective-permute-start
  525.1 118.8 %all-reduce.2.cloned.1.call-start = ((), (), s32[]{:S(2)}) async-start(), calls=%async_computation.2 | async-start | bytes 1048576 | tf_op jit(solution)/shard_map/while/body/eval_jaxpr/psum | solution.py:46
  644.0 7.3 copy-start.2
  646.0 6.9 collective-permute-start
  652.9 118.8 %all-reduce.2.cloned.1.call-start = ((), (), s32[]{:S(2)}) async-start(), calls=%async_computation.2 | async-start | bytes 1048576 | tf_op jit(solution)/shard_map/while/body/eval_jaxpr/psum | solution.py:46
  771.7 7.3 copy-start.2
  773.7 6.9 collective-permute-start
  780.6 119.1 %all-reduce.2.cloned.1.call-start = ((), (), s32[]{:S(2)}) async-start(), calls=%async_computation.2 | async-start | bytes 1048576 | tf_op jit(solution)/shard_map/while/body/eval_jaxpr/psum | solution.py:46
  899.8 7.3 copy-start.2
  901.8 6.9 collective-permute-start
  908.7 119.1 %all-reduce.2.cloned.1.call-start = ((), (), s32[]{:S(2)}) async-start(), calls=%async_computation.2 | async-start | bytes 1048576 | tf_op jit(solution)/shard_map/while/body/eval_jaxpr/psum | solution.py:46
  1027.8 7.3 copy-start.2
  1029.8 6.9 collective-permute-start
  1036.7 119.1 %all-reduce.2.cloned.1.call-start = ((), (), s32[]{:S(2)}) async-start(), calls=%async_computation.2 | async-start | bytes 1048576 | tf_op jit(solution)/shard_map/while/body/eval_jaxpr/psum | solution.py:46
  1155.9 7.3 copy-start.2
  1157.9 6.9 collective-permute-start
  1164.8 118.8 %all-reduce.2.cloned.1.call-start = ((), (), s32[]{:S(2)}) async-start(), calls=%async_computation.2 | async-start | bytes 1048576 | tf_op jit(solution)/shard_map/while/body/eval_jaxpr/psum | solution.py:46
  1283.6 7.3 copy-start.2
  1285.7 6.9 collective-permute-start
  1292.6 119.1 %all-reduce.2.cloned.1.call-start = ((), (), s32[]{:S(2)}) async-start(), calls=%async_computation.2 | async-start | bytes 1048576 | tf_op jit(solution)/shard_map/while/body/eval_jaxpr/psum | solution.py:46
  1411.7 7.3 copy-start.2
  1413.8 6.9 collective-permute-start
  1420.7 118.8 %all-reduce.2.cloned.1.call-start = ((), (), s32[]{:S(2)}) async-start(), calls=%async_computation.2 | async-start | bytes 1048576 | tf_op jit(solution)/shard_map/while/body/eval_jaxpr/psum | solution.py:46
  1539.5 7.3 copy-start.2
  1541.6 6.9 collective-permute-start
  1548.5 119.1 %all-reduce.2.cloned.1.call-start = ((), (), s32[]{:S(2)}) async-start(), calls=%async_computation.2 | async-start | bytes 1048576 | tf_op jit(solution)/shard_map/while/body/eval_jaxpr/psum | solution.py:46
  1667.6 7.3 copy-start.2
  1669.6 6.9 collective-permute-start
  1676.5 118.8 %all-reduce.2.cloned.1.call-start = ((), (), s32[]{:S(2)}) async-start(), calls=%async_computation.2 | async-start | bytes 1048576 | tf_op jit(solution)/shard_map/while/body/eval_jaxpr/psum | solution.py:46
  1795.3 7.3 copy-start.2
  1797.3 6.9 collective-permute-start
  1804.2 118.8 %all-reduce.2.cloned.1.call-start = ((), (), s32[]{:S(2)}) async-start(), calls=%async_computation.2 | async-start | bytes 1048576 | tf_op jit(solution)/shard_map/while/body/eval_jaxpr/psum | solution.py:46
  1923.1 7.3 copy-start.2
  1925.1 6.9 collective-permute-start
  1932.0 48.9 %reduce-scatter.2.cloned.1.call-start = ((), (), s32[]{:S(2)}) async-start(), calls=%async_computation.1 | async-start | bytes 2359296 | tf_op jit(solution)/shard_map/reduce_scatter | solution.py:74
  1936.5 0.9 copy-start.3
Sparse Core Ops, SparseCore 0:
  16.2 116.0 all-reduce.1
  145.2 115.0 all-reduce.1
  273.3 115.0 all-reduce.1
  401.1 115.0 all-reduce.1
  528.8 115.0 all-reduce.1
  656.6 115.0 all-reduce.1
  784.6 115.0 all-reduce.1
  912.7 115.0 all-reduce.1
  1040.8 115.0 all-reduce.1
  1168.5 115.0 all-reduce.1
  1296.6 115.0 all-reduce.1
  1424.4 115.0 all-reduce.1
  1552.5 115.0 all-reduce.1
  1680.2 115.0 all-reduce.1
  1807.9 115.0 all-reduce.1
Sparse Core Ops, SparseCore 1:
  1936.6 44.3 reduce-scatter.1
where the time goes:
time: 1990 us
  waiting for transfers between devices  1760 us (88%)
  local copies, waits for them, and re-layouts  66.1 us (3%)
  matrix products  51.9 us (3%)
  starting transfers between devices  51.8 us (3%)
  other arithmetic  42.9 us (2%)
    psum x15, waiting for transfers between devices, advance(): summed_all = lax.psum(partial_value, 'rows')  1720 us
    ppermute x15, starting transfers between devices, shifted(): return lax.ppermute(block, axis, route)  51.8 us
    reduce_scatter x1, waiting for transfers between devices, per_device(): lax.psum_scatter(tall_terms, 'panel', scatter_dimension=0, tiled=True)  43.4 us
  transfers between devices with their start and end apart: 31, of which 16 were waited for; matrix products, arithmetic and copies ran while one was open for 4% of the time, Pallas kernels for 0%

commit v1 on v0

--- a/solution.py
+++ b/solution.py
@@ -43,7 +43,7 @@
         reduced = (rhs_now - incoming).astype(jnp.bfloat16)
         partial_value = jnp.dot(inverse_cols, reduced, preferred_element_type=jnp.float32)
         partial_value = jnp.where(owner, partial_value, jnp.float32(0.0))
-        summed_all = lax.psum(partial_value, "rows")
+        summed_all = jnp.sum(lax.all_gather(partial_value, "rows"), axis=0)
         own_rows = lax.dynamic_slice_in_dim(summed_all, rows_index * slice_rows, slice_rows, 0)
         solved = summed_all.astype(jnp.bfloat16)
         previous = lax.dynamic_index_in_dim(solutions, batch_safe, 0, keepdims=False)

time: 1990 us -> 1830 us (0.920)
  waiting for transfers between devices: 1760 us -> 1250 us
  local copies, waits for them, and re-layouts: 66.1 us -> 307 us
  other arithmetic: 42.9 us -> 164 us
    psum x15 -> x0, waiting for transfers between devices: 1720 us -> none  [advance(): summed_all = lax.psum(partial_value, 'rows')]
    all_gather x0 -> x15, waiting for transfers between devices: none -> 1190 us  [advance(): summed_all = jnp.sum(lax.all_gather(partial_value, 'rows'), axis=0)]
    while x30 -> x15, local copies, waits for them, and re-layouts: 0.06 us -> 265 us
    reduce_sum x0 -> x15, other arithmetic: none -> 135 us  [advance(): summed_all = jnp.sum(lax.all_gather(partial_value, 'rows'), axis=0)]
  transfers between devices with their start and end apart: 31 -> 31, of which waited for: 16 -> 31; matrix products, arithmetic and copies ran while one was open for 4% -> 3% of each run, Pallas kernels for 0% -> 0%
where the time goes in v1:
time: 1830 us
  waiting for transfers between devices  1250 us (68%)
  local copies, waits for them, and re-layouts  307 us (17%)
  other arithmetic  164 us (9%)
  starting transfers between devices  52 us (3%)
  matrix products  41.4 us (2%)
    all_gather x15, waiting for transfers between devices, advance(): summed_all = jnp.sum(lax.all_gather(partial_value, 'rows'), axis=0)  1190 us
    while x15, local copies, waits for them, and re-layouts  265 us
    reduce_sum x15, other arithmetic, advance(): summed_all = jnp.sum(lax.all_gather(partial_value, 'rows'), axis=0)  135 us
    ppermute x15, starting transfers between devices, shifted(): return lax.ppermute(block, axis, route)  52 us
    reduce_scatter x1, waiting for transfers between devices, per_device(): lax.psum_scatter(tall_terms, 'panel', scatter_dimension=0, tiled=True)  43.2 us
  transfers between devices with their start and end apart: 31, of which 31 were waited for; matrix products, arithmetic and copies ran while one was open for 3% of the time, Pallas kernels for 0%

profile of v1, /device:TPU:2, one launch (start us, length us, event | category | flops | bytes accessed | tf_op | source)
XLA Modules:
  0.0 1828.6 jit_solution(2630523425063982597)
XLA Ops:
  12.1 1758.9 %while.19 = (s32[]{:T(128)}, f32[256,128]{0,1:T(8,128)S(1)}, f32[8,32,128]{2,1,0:T(8,128)}, bf16[8,1024,128]{1,2,0:T(8,128)(2,1)}, pred[]{:T(512)}, /*index=5*/p...) while((s32[]{:T(128)}, f32[256,128]{0,1:T(8,128)S(1)}, ...), condition=%wide.region_2.3_spmd, body=%wide.region_0.2_spmd.sunk | while | flops 138973184 | bytes 107331896 | solution.py:69
  15.1 81.0 %all-gather.5.cloned.1.call-done = f32[32768,128]{0,1:T(8,128)} async-done(((f32[1024,128]{0,1:T(8,128)}), f32[32768,128]{0,1:T(8,128)}) %all-gather.5.cloned.1.call-update) | async-done | bytes 16777232 | tf_op jit(solution)/shard_map/while/body/eval_jaxpr/all_gather | solution.py:46
  96.0 17.7 copy.26
  113.7 9.0 bitcast_reduce_fusion.2
  124.1 3.5 collective-permute-start
  133.6 79.7 %all-gather.5.cloned.1.call-done = f32[32768,128]{0,1:T(8,128)} async-done(((f32[1024,128]{0,1:T(8,128)}), f32[32768,128]{0,1:T(8,128)}) %all-gather.5.cloned.1.call-update) | async-done | bytes 16777232 | tf_op jit(solution)/shard_map/while/body/eval_jaxpr/all_gather | solution.py:46
  213.4 17.7 copy.26
  231.0 9.0 bitcast_reduce_fusion.2
  241.4 3.5 collective-permute-start
  244.9 1.7 fusion.28
  250.9 79.7 %all-gather.5.cloned.1.call-done = f32[32768,128]{0,1:T(8,128)} async-done(((f32[1024,128]{0,1:T(8,128)}), f32[32768,128]{0,1:T(8,128)}) %all-gather.5.cloned.1.call-update) | async-done | bytes 16777232 | tf_op jit(solution)/shard_map/while/body/eval_jaxpr/all_gather | solution.py:46
  330.7 17.7 copy.26
  348.4 9.0 bitcast_reduce_fusion.2
  358.7 3.5 collective-permute-start
  368.3 79.4 %all-gather.5.cloned.1.call-done = f32[32768,128]{0,1:T(8,128)} async-done(((f32[1024,128]{0,1:T(8,128)}), f32[32768,128]{0,1:T(8,128)}) %all-gather.5.cloned.1.call-update) | async-done | bytes 16777232 | tf_op jit(solution)/shard_map/while/body/eval_jaxpr/all_gather | solution.py:46
  447.7 17.7 copy.26
  465.4 9.0 bitcast_reduce_fusion.2
  475.7 3.5 collective-permute-start
  485.3 79.4 %all-gather.5.cloned.1.call-done = f32[32768,128]{0,1:T(8,128)} async-done(((f32[1024,128]{0,1:T(8,128)}), f32[32768,128]{0,1:T(8,128)}) %all-gather.5.cloned.1.call-update) | async-done | bytes 16777232 | tf_op jit(solution)/shard_map/while/body/eval_jaxpr/all_gather | solution.py:46
  564.7 17.7 copy.26
  582.4 9.0 bitcast_reduce_fusion.2
  592.7 3.5 collective-permute-start
  602.3 79.4 %all-gather.5.cloned.1.call-done = f32[32768,128]{0,1:T(8,128)} async-done(((f32[1024,128]{0,1:T(8,128)}), f32[32768,128]{0,1:T(8,128)}) %all-gather.5.cloned.1.call-update) | async-done | bytes 16777232 | tf_op jit(solution)/shard_map/while/body/eval_jaxpr/all_gather | solution.py:46
  681.7 17.7 copy.26
  699.4 9.0 bitcast_reduce_fusion.2
  709.7 3.5 collective-permute-start
  719.3 79.7 %all-gather.5.cloned.1.call-done = f32[32768,128]{0,1:T(8,128)} async-done(((f32[1024,128]{0,1:T(8,128)}), f32[32768,128]{0,1:T(8,128)}) %all-gather.5.cloned.1.call-update) | async-done | bytes 16777232 | tf_op jit(solution)/shard_map/while/body/eval_jaxpr/all_gather | solution.py:46
  799.0 17.7 copy.26
  816.7 9.0 bitcast_reduce_fusion.2
  827.1 3.5 collective-permute-start
  836.6 79.7 %all-gather.5.cloned.1.call-done = f32[32768,128]{0,1:T(8,128)} async-done(((f32[1024,128]{0,1:T(8,128)}), f32[32768,128]{0,1:T(8,128)}) %all-gather.5.cloned.1.call-update) | async-done | bytes 16777232 | tf_op jit(solution)/shard_map/while/body/eval_jaxpr/all_gather | solution.py:46
  916.4 17.7 copy.26
  934.0 9.0 bitcast_reduce_fusion.2
  944.4 3.5 collective-permute-start
  954.0 79.7 %all-gather.5.cloned.1.call-done = f32[32768,128]{0,1:T(8,128)} async-done(((f32[1024,128]{0,1:T(8,128)}), f32[32768,128]{0,1:T(8,128)}) %all-gather.5.cloned.1.call-update) | async-done | bytes 16777232 | tf_op jit(solution)/shard_map/while/body/eval_jaxpr/all_gather | solution.py:46
  1033.7 17.7 copy.26
  1051.4 9.0 bitcast_reduce_fusion.2
  1061.7 3.5 collective-permute-start
  1071.3 79.4 %all-gather.5.cloned.1.call-done = f32[32768,128]{0,1:T(8,128)} async-done(((f32[1024,128]{0,1:T(8,128)}), f32[32768,128]{0,1:T(8,128)}) %all-gather.5.cloned.1.call-update) | async-done | bytes 16777232 | tf_op jit(solution)/shard_map/while/body/eval_jaxpr/all_gather | solution.py:46
  1150.7 17.7 copy.26
  1168.4 9.0 bitcast_reduce_fusion.2
  1178.7 3.5 collective-permute-start
  1188.3 79.7 %all-gather.5.cloned.1.call-done = f32[32768,128]{0,1:T(8,128)} async-done(((f32[1024,128]{0,1:T(8,128)}), f32[32768,128]{0,1:T(8,128)}) %all-gather.5.cloned.1.call-update) | async-done | bytes 16777232 | tf_op jit(solution)/shard_map/while/body/eval_jaxpr/all_gather | solution.py:46
  1268.0 17.7 copy.26
  1285.7 9.0 bitcast_reduce_fusion.2
  1296.0 3.5 collective-permute-start
  1305.6 79.4 %all-gather.5.cloned.1.call-done = f32[32768,128]{0,1:T(8,128)} async-done(((f32[1024,128]{0,1:T(8,128)}), f32[32768,128]{0,1:T(8,128)}) %all-gather.5.cloned.1.call-update) | async-done | bytes 16777232 | tf_op jit(solution)/shard_map/while/body/eval_jaxpr/all_gather | solution.py:46
  1385.0 17.7 copy.26
  1402.7 9.0 bitcast_reduce_fusion.2
  1413.0 3.5 collective-permute-start
  1422.6 79.7 %all-gather.5.cloned.1.call-done = f32[32768,128]{0,1:T(8,128)} async-done(((f32[1024,128]{0,1:T(8,128)}), f32[32768,128]{0,1:T(8,128)}) %all-gather.5.cloned.1.call-update) | async-done | bytes 16777232 | tf_op jit(solution)/shard_map/while/body/eval_jaxpr/all_gather | solution.py:46
  1502.3 17.7 copy.26
  1520.0 9.0 bitcast_reduce_fusion.2
  1530.4 3.5 collective-permute-start
  1539.9 79.4 %all-gather.5.cloned.1.call-done = f32[32768,128]{0,1:T(8,128)} async-done(((f32[1024,128]{0,1:T(8,128)}), f32[32768,128]{0,1:T(8,128)}) %all-gather.5.cloned.1.call-update) | async-done | bytes 16777232 | tf_op jit(solution)/shard_map/while/body/eval_jaxpr/all_gather | solution.py:46
  1619.3 17.7 copy.26
  1637.0 9.0 bitcast_reduce_fusion.2
  1647.4 3.5 collective-permute-start
  1656.9 79.4 %all-gather.5.cloned.1.call-done = f32[32768,128]{0,1:T(8,128)} async-done(((f32[1024,128]{0,1:T(8,128)}), f32[32768,128]{0,1:T(8,128)}) %all-gather.5.cloned.1.call-update) | async-done | bytes 16777232 | tf_op jit(solution)/shard_map/while/body/eval_jaxpr/all_gather | solution.py:46
  1736.4 17.7 copy.26
  1754.0 9.0 bitcast_reduce_fusion.2
  1764.4 3.5 collective-permute-start
  1771.0 4.5 multiply_bitcast_fusion
  1776.5 43.2 %reduce-scatter.2.cloned.1.call-done = f32[1,512,128]{1,2,0:T(8,128)} async-done(((f32[8,512,128]{1,2,0:T(8,128)}), f32[1,512,128]{1,2,0:T(8,128)}) %reduce-scatter.2.cloned.1.call-update) | async-done | bytes 262160 | tf_op jit(solution)/shard_map/reduce_scatter | solution.py:74
  (209 shorter events, 116.2 us)
Async XLA Ops:
  8.0 1.6 copy-start
  12.1 83.9 %all-gather.5.cloned.1.call-start = ((), (), s32[]{:S(2)}) async-start(), calls=%async_computation.2 | async-start | bytes 17301504 | tf_op jit(solution)/shard_map/while/body/eval_jaxpr/all_gather | solution.py:46
  124.1 6.6 collective-permute-start
  130.7 82.7 %all-gather.5.cloned.1.call-start = ((), (), s32[]{:S(2)}) async-start(), calls=%async_computation.2 | async-start | bytes 17301504 | tf_op jit(solution)/shard_map/while/body/eval_jaxpr/all_gather | solution.py:46
  241.4 6.6 collective-permute-start
  248.0 82.6 %all-gather.5.cloned.1.call-start = ((), (), s32[]{:S(2)}) async-start(), calls=%async_computation.2 | async-start | bytes 17301504 | tf_op jit(solution)/shard_map/while/body/eval_jaxpr/all_gather | solution.py:46
  358.7 6.6 collective-permute-start
  365.3 82.3 %all-gather.5.cloned.1.call-start = ((), (), s32[]{:S(2)}) async-start(), calls=%async_computation.2 | async-start | bytes 17301504 | tf_op jit(solution)/shard_map/while/body/eval_jaxpr/all_gather | solution.py:46
  475.7 6.6 collective-permute-start
  482.4 82.3 %all-gather.5.cloned.1.call-start = ((), (), s32[]{:S(2)}) async-start(), calls=%async_computation.2 | async-start | bytes 17301504 | tf_op jit(solution)/shard_map/while/body/eval_jaxpr/all_gather | solution.py:46
  592.7 6.6 collective-permute-start
  599.4 82.3 %all-gather.5.cloned.1.call-start = ((), (), s32[]{:S(2)}) async-start(), calls=%async_computation.2 | async-start | bytes 17301504 | tf_op jit(solution)/shard_map/while/body/eval_jaxpr/all_gather | solution.py:46
  709.7 6.6 collective-permute-start
  716.4 82.7 %all-gather.5.cloned.1.call-start = ((), (), s32[]{:S(2)}) async-start(), calls=%async_computation.2 | async-start | bytes 17301504 | tf_op jit(solution)/shard_map/while/body/eval_jaxpr/all_gather | solution.py:46
  827.1 6.6 collective-permute-start
  833.7 82.7 %all-gather.5.cloned.1.call-start = ((), (), s32[]{:S(2)}) async-start(), calls=%async_computation.2 | async-start | bytes 17301504 | tf_op jit(solution)/shard_map/while/body/eval_jaxpr/all_gather | solution.py:46
  944.4 6.6 collective-permute-start
  951.0 82.6 %all-gather.5.cloned.1.call-start = ((), (), s32[]{:S(2)}) async-start(), calls=%async_computation.2 | async-start | bytes 17301504 | tf_op jit(solution)/shard_map/while/body/eval_jaxpr/all_gather | solution.py:46
  1061.7 6.6 collective-permute-start
  1068.3 82.3 %all-gather.5.cloned.1.call-start = ((), (), s32[]{:S(2)}) async-start(), calls=%async_computation.2 | async-start | bytes 17301504 | tf_op jit(solution)/shard_map/while/body/eval_jaxpr/all_gather | solution.py:46
  1178.7 6.6 collective-permute-start
  1185.3 82.6 %all-gather.5.cloned.1.call-start = ((), (), s32[]{:S(2)}) async-start(), calls=%async_computation.2 | async-start | bytes 17301504 | tf_op jit(solution)/shard_map/while/body/eval_jaxpr/all_gather | solution.py:46
  1296.0 6.6 collective-permute-start
  1302.7 82.3 %all-gather.5.cloned.1.call-start = ((), (), s32[]{:S(2)}) async-start(), calls=%async_computation.2 | async-start | bytes 17301504 | tf_op jit(solution)/shard_map/while/body/eval_jaxpr/all_gather | solution.py:46
  1413.0 6.6 collective-permute-start
  1419.7 82.7 %all-gather.5.cloned.1.call-start = ((), (), s32[]{:S(2)}) async-start(), calls=%async_computation.2 | async-start | bytes 17301504 | tf_op jit(solution)/shard_map/while/body/eval_jaxpr/all_gather | solution.py:46
  1530.4 6.6 collective-permute-start
  1537.0 82.3 %all-gather.5.cloned.1.call-start = ((), (), s32[]{:S(2)}) async-start(), calls=%async_computation.2 | async-start | bytes 17301504 | tf_op jit(solution)/shard_map/while/body/eval_jaxpr/all_gather | solution.py:46
  1647.4 6.6 collective-permute-start
  1654.0 82.3 %all-gather.5.cloned.1.call-start = ((), (), s32[]{:S(2)}) async-start(), calls=%async_computation.2 | async-start | bytes 17301504 | tf_op jit(solution)/shard_map/while/body/eval_jaxpr/all_gather | solution.py:46
  1764.4 6.6 collective-permute-start
  1771.0 48.6 %reduce-scatter.2.cloned.1.call-start = ((), (), s32[]{:S(2)}) async-start(), calls=%async_computation.1 | async-start | bytes 2359296 | tf_op jit(solution)/shard_map/reduce_scatter | solution.py:74
  1775.5 0.9 copy-start.1
Sparse Core Ops, SparseCore 0:
  15.6 80.4 all-gather.4
  134.1 79.1 all-gather.4
  251.4 79.1 all-gather.4
  368.4 79.1 all-gather.4
  485.5 79.1 all-gather.4
  602.5 79.1 all-gather.4
  719.8 79.1 all-gather.4
  837.1 79.1 all-gather.4
  954.4 79.1 all-gather.4
  1071.4 79.1 all-gather.4
  1188.8 79.1 all-gather.4
  1305.8 79.1 all-gather.4
  1423.1 79.1 all-gather.4
  1540.1 79.1 all-gather.4
  1657.1 79.1 all-gather.4
Sparse Core Ops, SparseCore 1:
  1775.6 44.0 reduce-scatter.1
